TPU v7x, 32 devices: a whole 2x2x4 slice. The times are simulated.
32 devices in a mesh: rows: 8 (over y, x, core), cols: 4 (over z).
Axes of the slice: x: 2, y: 2, z: 4, core: 2. Of those that a mesh axis runs over, the one named last changes fastest.
Arguments:
- grads: bfloat16 [9216, 8192], P(('rows', 'cols')), may hold values from -6 to 6
- tests: float32 [64, 8192], P(None, 'cols'), may hold values from -6 to 6
Outputs:
- solution: float32 [64, 8192], P(None, 'cols')
- scores: float32 [64, 9216], P(None, ('rows', 'cols'))
All inputs are finite; a program needn't handle non-finite values.
Results may differ from a plain program's by a relative error of at most 0.0041.
Values may be sent and summed in bfloat16 or wider, within the bound.
A program may use at most 64 MiB of HBM per device.

v0:
```python
import jax
import jax.numpy as jnp
from jax import lax
from jax.sharding import PartitionSpec as P

damping = 0.5


def per_device(grads, tests):
    n_total = grads.shape[0] * lax.axis_size("rows") * lax.axis_size("cols")
    width = grads.shape[1]
    own = tests.shape[1]
    direction = lax.all_gather(tests, "cols", axis=1, tiled=True)
    norm_now = jnp.sum(direction * direction, axis=1)

    def project(d):
        return lax.dot_general(
            grads,
            d.astype(jnp.bfloat16),
            (((1,), (1,)), ((), ())),
            preferred_element_type=jnp.float32,
        )

    partial_value = lax.dot_general(
        project(direction).astype(jnp.bfloat16),
        grads,
        (((0,), (0,)), ((), ())),
        preferred_element_type=jnp.float32,
    )
    image = lax.psum(partial_value, ("rows", "cols")) / n_total + damping * direction
    alpha = norm_now / jnp.sum(direction * image, axis=1)
    solution = alpha[:, None] * direction
    residual = direction - alpha[:, None] * image
    norm_next = jnp.sum(residual * residual, axis=1)
    direction = residual + (norm_next / norm_now)[:, None] * direction
    proj = project(direction)
    curv = lax.psum(
        jnp.sum(proj * proj.astype(jnp.bfloat16).astype(jnp.float32), axis=0), ("rows", "cols")
    )
    curv = curv / n_total + damping * jnp.sum(direction * direction, axis=1)
    solution = solution + (norm_next / curv)[:, None] * direction
    scores = lax.dot_general(
        solution.astype(jnp.bfloat16),
        grads,
        (((1,), (1,)), ((), ())),
        preferred_element_type=jnp.float32,
    )
    mine = lax.dynamic_slice_in_dim(solution, lax.axis_index("cols") * own, own, axis=1)
    return (mine, scores * width ** (-0.5))


def solution(mesh):
    placed = (P(("rows", "cols"), None), P(None, "cols"))
    return jax.shard_map(
        per_device,
        mesh=mesh,
        in_specs=placed,
        out_specs=(P(None, "cols"), P(None, ("rows", "cols"))),
        check_vma=False,
    )
```

profile of v0, /device:TPU:0, one launch (start us, length us, event | category | flops | bytes accessed | tf_op | source)
XLA Modules:
  0.0 261.7 jit_solution(16199284651384448593)
XLA Ops:
  7.2 0.0 all-gather.2.cloned.1.call-start
  7.2 0.7 all-gather.2.cloned.1.call-update
  7.9 0.0 all-reduce.2.cloned.1.call-start
  7.9 50.0 %all-gather.2.cloned.1.call-done = f32[64,8192]{1,0:T(8,128)} async-done(((f32[64,2048]{1,0:T(8,128)}), f32[64,8192]{1,0:T(8,128)}) %all-gather.2.cloned.1.call-update) | async-done | bytes 2097168 | tf_op jit(solution)/shard_map/all_gather | solution.py:13
  58.0 9.7 %fusion = f32[64,8192]{1,0:T(8,128)} fusion(bf16[288,8192]{1,0:T(8,128)(2,1)} %param.2, f32[64,8192]{1,0:T(8,128)} %all-gather.2.cloned.1.call-done), kind=kOutput, calls=%fused_computation.11 | convolution fusion | flops 604522496 | bytes 8912896 | tf_op jit(solution)/shard_map/dot_general | solution.py:24
  67.6 0.0 copy-start
  67.6 0.0 all-reduce.2.cloned.1.call-update
  67.7 133.7 %all-reduce.2.cloned.1.call-done = f32[64,8192]{1,0:T(8,128)} async-done(((f32[64,8192]{1,0:T(8,128)}), f32[64,8192]{1,0:T(8,128)}) %all-reduce.2.cloned.1.call-update) | async-done | bytes 2097168 | tf_op jit(solution)/shard_map/psum | solution.py:30
  201.4 0.0 copy-done
  201.4 0.0 copy-start.1
  201.4 2.3 multiply_reduce_fusion.2
  203.7 0.0 copy-start.2
  203.7 2.3 multiply_reduce_fusion.1
  206.1 0.0 copy-done.1
  206.1 0.0 copy-done.2
  206.1 0.0 slice-start
  206.1 1.8 multiply_reduce_fusion.4
  207.9 38.9 %psum.15 = f32[64]{0:T(128)S(1)} all-reduce(f32[64]{0:T(128)S(1)} %multiply_reduce_fusion.4), channel_id=1, replica_groups=mesh['rows'=8,'cols'=4] {'rows','cols'}, use_global_device_ids=true, to_apply=%region_5.0 | all-reduce | flops 64 | bytes 512 | tf_op jit(solution)/shard_map/psum | solution.py:37
  246.9 0.0 slice-start.1
  246.9 2.5 multiply_reduce_fusion
  249.4 2.3 multiply_add_fusion
  251.7 0.0 slice-done
  251.7 0.0 slice-done.1
  251.7 2.3 convolution_multiply_fusion
  254.0 0.8 constant_dynamic-slice_fusion
  (4 shorter events, 0.0 us)
Async XLA Ops:
  7.2 50.8 %all-gather.2.cloned.1.call-start = ((), (), s32[]{:S(2)}) async-start(), calls=%async_computation | async-start | bytes 2621440 | tf_op jit(solution)/shard_map/all_gather | solution.py:13
  7.9 193.5 %all-reduce.2.cloned.1.call-start = ((), (), s32[]{:S(2)}) async-start(), calls=%async_computation.1 | async-start | bytes 4194304 | tf_op jit(solution)/shard_map/psum | solution.py:30
  67.6 133.7 %copy-start = (f32[64,8192]{1,0:T(8,128)S(1)}, f32[64,8192]{1,0:T(8,128)}, u32[]{:S(2)}) copy-start(f32[64,8192]{1,0:T(8,128)} %all-gather.2.cloned.1.call-done) | copy-start | bytes 6291460
  201.4 4.7 %copy-start.1 = (bf16[288,8192]{1,0:T(8,128)(2,1)S(1)}, bf16[288,8192]{1,0:T(8,128)(2,1)}, u32[]{:S(2)}) copy-start(bf16[288,8192]{1,0:T(8,128)(2,1)} %param.2) | copy-start | bytes 14155780
  203.7 2.4 copy-start.2
  206.1 45.6 %slice-start = ((s8[4718592]{0:T(1024)(128)(4,1)}), s8[524288]{0:T(1024)(128)(4,1)S(1)}, s32[]{:S(2)}) async-start(s8[4718592]{0:T(1024)(128)(4,1)} %bitcast.8), calls=%async_computation.2 | async-start | bytes 1048576
  246.9 4.8 %slice-start.1 = ((s8[4718592]{0:T(1024)(128)(4,1)}), s8[4194304]{0:T(1024)(128)(4,1)S(1)}, s32[]{:S(2)}) async-start(s8[4718592]{0:T(1024)(128)(4,1)} %bitcast.8), calls=%async_computation.3 | async-start | bytes 8388608
Sparse Core Ops, SparseCore 0:
  9.5 48.3 all-gather.1
  67.8 133.5 all-reduce.1
where the time goes:
time: 262 us
  waiting for transfers between devices  184 us (70%)
  blocking collectives  38.9 us (15%)
  between operations  14.1 us (5%)
  matrix products  13.8 us (5%)
  other arithmetic  9.47 us (4%)
    psum x1, waiting for transfers between devices, per_device(): lax.psum(partial_value, ('rows', 'cols')) / n_total + damping * direction  134 us
    all_gather x1, waiting for transfers between devices, per_device(): direction = lax.all_gather(tests, 'cols', axis=1, tiled=True)  50 us
    psum x1, blocking collectives, per_device(): lax.psum(jnp.sum(proj * proj.astype(jnp.bfloat16).astype(jnp.float32), ax...  38.9 us
    dot_general x1, matrix products, per_device(): lax.dot_general(project(direction).astype(jnp.bfloat16), grads, (((0,), (...  9.67 us
  transfers between devices with their start and end apart: 2, of which 2 were waited for; matrix products, arithmetic and copies ran while one was open for 0% of the time, Pallas kernels for 0%

commit v1 on v0

--- a/solution.py
+++ b/solution.py
@@ -6,11 +6,33 @@
 damping = 0.5
 
 
+def laid_out(pieces, dim):
+    dims = list(pieces.shape[1:])
+    dims[dim] *= pieces.shape[0]
+    return jnp.moveaxis(pieces, 0, dim).reshape(dims)
+
+
+def grow_blocks(shard, axis):
+    peers = lax.axis_size(axis)
+    blocks = shard[None]
+    for level in range(peers.bit_length() - 1):
+        bit = 1 << level
+        other = lax.ppermute(blocks, axis, [(i, i ^ bit) for i in range(peers)])
+        both = jnp.stack([blocks, other])
+        upper = lax.axis_index(axis) >> level & 1
+        blocks = jnp.where(upper == 0, both, both[::-1]).reshape(-1, *shard.shape)
+    return blocks
+
+
+def gather_by_bits(shard, axis, dim):
+    return laid_out(grow_blocks(shard, axis), dim)
+
+
 def per_device(grads, tests):
     n_total = grads.shape[0] * lax.axis_size("rows") * lax.axis_size("cols")
     width = grads.shape[1]
     own = tests.shape[1]
-    direction = lax.all_gather(tests, "cols", axis=1, tiled=True)
+    direction = gather_by_bits(tests, "cols", 1)
     norm_now = jnp.sum(direction * direction, axis=1)
 
     def project(d):

time: 262 us -> 282 us (1.076)
  waiting for transfers between devices: 184 us -> 190 us
  starting transfers between devices: 0.08 us -> 5.97 us
  matrix products: 13.8 us -> 18 us
    ppermute x0 -> x2, waiting for transfers between devices: none -> 57.1 us  [grow_blocks(): other = lax.ppermute(blocks, axis, [(i, i ^ bit) for i in range(peers)])]
    all_gather x1 -> x0, waiting for transfers between devices: 50 us -> none  [per_device(): direction = lax.all_gather(tests, 'cols', axis=1, tiled=True)]
    ppermute x0 -> x2, starting transfers between devices: none -> 5.94 us  [grow_blocks(): other = lax.ppermute(blocks, axis, [(i, i ^ bit) for i in range(peers)])]
    reduce_sum x0 -> x1, other arithmetic: none -> 3.15 us  [per_device(): norm_now = jnp.sum(direction * direction, axis=1)]
  transfers between devices with their start and end apart: 2 -> 3, of which waited for: 2 -> 3; matrix products, arithmetic and copies ran while one was open for 0% -> 1% of each run, Pallas kernels for 0% -> 0%
where the time goes in v1:
time: 282 us; the launch traced here: 281 us
  waiting for transfers between devices  190 us (67%)
  blocking collectives  39.1 us (14%)
  matrix products  18 us (6%)
  between operations  14.1 us (5%)
  other arithmetic  11 us (4%)
  starting transfers between devices  5.97 us (2%)
  local copies, waits for them, and re-layouts  3.41 us (1%)
    psum x1, waiting for transfers between devices, per_device(): lax.psum(partial_value, ('rows', 'cols')) / n_total + damping * direction  133 us
    ppermute x2, waiting for transfers between devices, grow_blocks(): other = lax.ppermute(blocks, axis, [(i, i ^ bit) for i in range(peers)])  57.1 us
    psum x1, blocking collectives, per_device(): lax.psum(jnp.sum(proj * proj.astype(jnp.bfloat16).astype(jnp.float32), ax...  39.1 us
    dot_general x1, matrix products, per_device(): lax.dot_general(project(direction).astype(jnp.bfloat16), grads, (((0,), (...  9.23 us
    ppermute x2, starting transfers between devices, grow_blocks(): other = lax.ppermute(blocks, axis, [(i, i ^ bit) for i in range(peers)])  5.94 us
  transfers between devices with their start and end apart: 3, of which 3 were waited for; matrix products, arithmetic and copies ran while one was open for 1% of the time, Pallas kernels for 0%

profile of v1, /device:TPU:0, one launch (start us, length us, event | category | flops | bytes accessed | tf_op | source)
XLA Modules:
  0.0 281.4 jit_solution(2368959386913164923)
XLA Ops:
  7.2 0.0 all-reduce.2.cloned.1.call-start
  7.2 3.1 %collective-permute-start = (f32[1,64,2048]{2,1,0:T(8,128)}, f32[1,64,2048]{2,1,0:T(8,128)S(1)}, u32[]{:S(2)}, u32[]{:S(2)}) collective-permute-start(f32[1,64,2048]{2,1,0:T(8,128)} %bitcast.33), channel_id=1, source_target_pairs={{0,1},{1,0},{2,3},{3,2},{4,5},{5,4},{6,7},{7,6},{8,9},{9,8},{10,11... | collective-permute-start | bytes 1572872 | tf_op jit(solution)/shard_map/ppermute | solution.py:20
  10.3 12.1 %collective-permute-done = f32[1,64,2048]{2,1,0:T(8,128)S(1)} collective-permute-done((f32[1,64,2048]{2,1,0:T(8,128)}, f32[1,64,2048]{2,1,0:T(8,128)S(1)}, u32[]{:S(2)}, u32[]{:S(2)}) %collective-permute-start) | collective-permute-done | bytes 524320 | tf_op jit(solution)/shard_map/ppermute | solution.py:20
  22.5 1.1 pad_maximum_fusion.1
  23.6 0.2 fusion.7
  23.8 2.8 %collective-permute-start.1 = (f32[2,64,2048]{2,1,0:T(8,128)S(1)}, f32[2,64,2048]{2,1,0:T(8,128)S(1)}, u32[]{:S(2)}, u32[]{:S(2)}) collective-permute-start(f32[2,64,2048]{2,1,0:T(8,128)S(1)} %get-tuple-element.3), channel_id=1, source_target_pairs={{0,2},{1,3},{2,0},{3,1},{4,6},{5,7},{6,4},{7,5},{8,10},{9,11},{10,... | collective-permute-start | bytes 3145736 | tf_op jit(solution)/shard_map/ppermute | solution.py:20
  26.6 44.9 %collective-permute-done.1 = f32[2,64,2048]{2,1,0:T(8,128)S(1)} collective-permute-done((f32[2,64,2048]{2,1,0:T(8,128)S(1)}, f32[2,64,2048]{2,1,0:T(8,128)S(1)}, u32[]{:S(2)}, u32[]{:S(2)}) %collective-permute-start.1) | collective-permute-done | bytes 1048608 | tf_op jit(solution)/shard_map/ppermute | solution.py:20
  71.6 0.2 pad_maximum_fusion
  71.8 0.2 reverse_select_fusion
  72.0 0.0 copy-start.2
  72.0 1.4 copy.4
  73.4 0.0 copy-done.2
  73.4 1.2 copy.5
  74.6 9.2 %fusion.1 = f32[64,8192]{1,0:T(8,128)} fusion(bf16[288,8192]{1,0:T(8,128)(2,1)} %param.2, f32[64,8192]{1,0:T(8,128)S(1)} %bitcast.23), kind=kOutput, calls=%fused_computation.15 | convolution fusion | flops 604522496 | bytes 8912896 | tf_op jit(solution)/shard_map/dot_general | solution.py:46
  83.8 0.0 all-reduce.2.cloned.1.call-update
  83.8 3.2 %fusion = f32[64]{0:T(128)S(1)} fusion(f32[4,64,2048]{2,1,0:T(8,128)} %bitcast.30), kind=kLoop, calls=%fused_computation.3 | loop fusion | flops 1048512 | bytes 2097408 | tf_op jit(solution)/shard_map/reduce_sum | solution.py:36
  87.0 132.6 %all-reduce.2.cloned.1.call-done = f32[64,8192]{1,0:T(8,128)} async-done(((f32[64,8192]{1,0:T(8,128)}), f32[64,8192]{1,0:T(8,128)}) %all-reduce.2.cloned.1.call-update) | async-done | bytes 2097168 | tf_op jit(solution)/shard_map/psum | solution.py:52
  219.6 0.0 copy-start
  219.6 2.2 multiply_reduce_fusion.2
  221.8 0.0 copy-done
  221.8 0.7 multiply_reduce_fusion.1
  222.5 4.2 %multiply_reduce_fusion.3 = f32[64]{0:T(128)S(1)} fusion(bf16[288,8192]{1,0:T(8,128)(2,1)} %param.2, f32[64,8192]{1,0:T(8,128)S(1)} %bitcast.26, f32[64,8192]{1,0:T(8,128)S(1)} %copy-done, f32[64]{0:T(128)S(1)} %div.32, f32[64]{0:T(128)S(1)} %div.31), kind=kOutput, calls=%fused_computation.22 | convolution fusion | flops 306257856 | bytes 8913664 | tf_op jit(solution)/shard_map/dot_general | solution.py:39
  226.7 39.1 %psum.15 = f32[64]{0:T(128)S(1)} all-reduce(f32[64]{0:T(128)S(1)} %multiply_reduce_fusion.3), channel_id=1, replica_groups=mesh['rows'=8,'cols'=4] {'rows','cols'}, use_global_device_ids=true, to_apply=%region_5.6 | all-reduce | flops 64 | bytes 512 | tf_op jit(solution)/shard_map/psum | solution.py:59
  265.8 0.0 copy-start.1
  265.8 2.5 multiply_reduce_fusion
  268.3 0.0 copy-done.1
  268.3 0.7 multiply_add_fusion
  269.1 4.6 %convolution_multiply_fusion = f32[64,288]{1,0:T(8,128)} fusion(bf16[288,8192]{1,0:T(8,128)(2,1)} %param.2, f32[64,8192]{1,0:T(8,128)S(1)} %multiply_add_fusion), kind=kOutput, calls=%fused_computation.12 | convolution fusion | flops 302532608 | bytes 6889472 | tf_op jit(solution)/shard_map/dot_general | solution.py:64
  273.7 0.8 constant_dynamic-slice_fusion
  (3 shorter events, 0.0 us)
Async XLA Ops:
  7.2 212.4 %all-reduce.2.cloned.1.call-start = ((), (), s32[]{:S(2)}) async-start(), calls=%async_computation | async-start | bytes 4194304 | tf_op jit(solution)/shard_map/psum | solution.py:52
  7.2 15.3 %collective-permute-start = (f32[1,64,2048]{2,1,0:T(8,128)}, f32[1,64,2048]{2,1,0:T(8,128)S(1)}, u32[]{:S(2)}, u32[]{:S(2)}) collective-permute-start(f32[1,64,2048]{2,1,0:T(8,128)} %bitcast.33), channel_id=1, source_target_pairs={{0,1},{1,0},{2,3},{3,2},{4,5},{5,4},{6,7},{7,6},{8,9},{9,8},{10,11... | collective-permute-start | bytes 1572872 | tf_op jit(solution)/shard_map/ppermute | solution.py:20
  23.8 47.8 %collective-permute-start.1 = (f32[2,64,2048]{2,1,0:T(8,128)S(1)}, f32[2,64,2048]{2,1,0:T(8,128)S(1)}, u32[]{:S(2)}, u32[]{:S(2)}) collective-permute-start(f32[2,64,2048]{2,1,0:T(8,128)S(1)} %get-tuple-element.3), channel_id=1, source_target_pairs={{0,2},{1,3},{2,0},{3,1},{4,6},{5,7},{6,4},{7,5},{8,10},{9,11},{10,... | collective-permute-start | bytes 3145736 | tf_op jit(solution)/shard_map/ppermute | solution.py:20
  72.0 1.4 copy-start.2
  219.6 2.2 copy-start
  265.8 2.5 copy-start.1
Sparse Core Ops, SparseCore 0:
  84.0 135.6 all-reduce.1
